TPU v7x, 32 devices: a whole 2x2x4 slice. The times are simulated.
32 devices in a mesh: tm: 16 (over z, y, x), rows: 2 (over core).
Axes of the slice: x: 2, y: 2, z: 4, core: 2. Of those that a mesh axis runs over, the one named last changes fastest.
Arguments:
- latents: bfloat16 [64, 8, 5120], P('tm', 'rows'), may hold values from -25 to 25
- cotangent: bfloat16 [64, 8, 5120], P('tm', 'rows'), may hold values from -6 to 6
- kernel_one: bfloat16 [3, 3, 3, 64, 64], replicated, may hold values from -0.15625 to 0.15625
- kernel_two: bfloat16 [3, 3, 3, 64, 64], replicated, may hold values from -0.15625 to 0.15625
- gain_one: float32 [64], replicated, may hold values from 0.5 to 1.5
- offset_one: float32 [64], replicated, may hold values from -3 to 3
- gain_two: float32 [64], replicated, may hold values from 0.5 to 1.5
- offset_two: float32 [64], replicated, may hold values from -3 to 3
- clip_id: int32 [64], P('tm'), may hold values from 0 to 7, never falling along the last dimension, each value on 1 to 16 neighbouring positions
Outputs:
- output: bfloat16 [64, 8, 5120], P('tm', 'rows')
- grad_latent: bfloat16 [64, 8, 5120], P('tm', 'rows')
- grad_kernel_one: float32 [3, 3, 3, 64, 64], replicated
- grad_kernel_two: float32 [3, 3, 3, 64, 64], replicated
Inputs may be any that keep to these rules, and one draw needn't show every extreme that they name: `clip_id`: clip numbers never fall along the frames; each clip number 0 to 7 names 1 to 16 consecutive frames, and one clip has exactly 16.
All inputs are finite; a program needn't handle non-finite values.
Results may differ from a plain program's by a relative error of at most 0.0085.
Values may be sent and summed in bfloat16 or wider, within the bound.
A program may use at most 128 MiB of HBM per device.

v0:
```python
import jax
import jax.numpy as jnp
from jax import lax
from jax.sharding import PartitionSpec as P

GROUPS = 32
EPSILON = 1e-06
HIGHEST = lax.Precision.HIGHEST


def with_halo(block, sides, width):
    for axis, dim in sides:
        count = lax.axis_size(axis)
        forward = [(i, i + 1) for i in range(count - 1)]
        backward = [(target, source) for source, target in forward]
        low = lax.ppermute(
            lax.slice_in_dim(block, block.shape[dim] - width, None, axis=dim), axis, forward
        )
        high = lax.ppermute(lax.slice_in_dim(block, 0, width, axis=dim), axis, backward)
        block = jnp.concatenate([low, block, high], axis=dim)
    return block


def passed_along(value, axis, by):
    length = lax.axis_size(axis)
    pairs = [(i, i + by) for i in range(length) if 0 <= i + by < length]
    return lax.ppermute(value, axis, pairs)


def row_halo(extended):
    return with_halo(extended, (("rows", 1),), 1)


def spread(extended, channels):
    depth, height, flat = extended.shape
    shaped = extended.reshape(depth, height, flat // channels, channels)
    return jnp.pad(shaped, ((0, 0), (0, 0), (1, 1), (0, 0)))


def forward_taps(frames, n_rows, n_cols):
    taps = [
        frames[:, row_tap : row_tap + n_rows, col_tap : col_tap + n_cols]
        for row_tap in range(3)
        for col_tap in range(3)
    ]
    joined = jnp.concatenate(taps, axis=-1)
    return joined.reshape(-1, joined.shape[-1])


def reverse_taps(frames, n_rows, n_cols):
    taps = [
        frames[:, 2 - row_tap : 2 - row_tap + n_rows, 2 - col_tap : 2 - col_tap + n_cols]
        for row_tap in range(3)
        for col_tap in range(3)
    ]
    joined = jnp.concatenate(taps, axis=-1)
    return joined.reshape(-1, joined.shape[-1])


def causal_conv(field, tags, kernel):
    n_frames, n_rows, flat = field.shape
    channels = kernel.shape[3]
    n_cols = flat // channels
    past_field, past_tags = passed_along((field[-2:], tags[-2:]), "tm", 1)
    padded = spread(row_halo(jnp.concatenate([past_field, field], axis=0)), channels)
    all_tags = jnp.concatenate([past_tags, tags])
    result = jnp.zeros((n_frames * n_rows * n_cols, kernel.shape[4]), jnp.float32)
    patch_list = []
    for lag in range(3):
        lag_mask = (all_tags[2 - lag : 2 - lag + n_frames] == tags).astype(jnp.bfloat16)
        frames = padded[2 - lag : 2 - lag + n_frames] * lag_mask[:, None, None, None]
        patches = forward_taps(frames, n_rows, n_cols)
        patch_list.append(patches)
        result = result + jnp.dot(
            patches, kernel[lag].reshape(-1, kernel.shape[4]), preferred_element_type=jnp.float32
        )
    return (result.reshape(n_frames, n_rows, flat), patch_list)


def transposed_conv(grad, tags, kernel):
    n_frames, n_rows, flat = grad.shape
    channels = kernel.shape[3]
    n_cols = flat // channels
    next_grad, next_tags = passed_along((grad[:2], tags[:2]), "tm", -1)
    padded = spread(row_halo(jnp.concatenate([grad, next_grad], axis=0)), channels)
    all_tags = jnp.concatenate([tags, next_tags])
    result = jnp.zeros((n_frames * n_rows * n_cols, channels), jnp.float32)
    for lag in range(3):
        lag_mask = (all_tags[lag : lag + n_frames] == tags).astype(jnp.bfloat16)
        frames = padded[lag : lag + n_frames] * lag_mask[:, None, None, None]
        patches = reverse_taps(frames, n_rows, n_cols)
        flipped = jnp.swapaxes(kernel[lag], 2, 3).reshape(-1, channels)
        result = result + jnp.dot(patches, flipped, preferred_element_type=jnp.float32)
    return result.reshape(n_frames, n_rows, flat)


def kernel_grad(patch_list, grad, channels):
    flat_grad = grad.reshape(-1, channels)
    stacked = [
        lax.dot_general(
            patches, flat_grad, (((0,), (0,)), ((), ())), preferred_element_type=jnp.float32
        ).reshape(3, 3, channels, channels)
        for patches in patch_list
    ]
    return jnp.stack(stacked)


def clip_totals(first, second, ones_col, clip_id):
    clips = lax.axis_size("tm") // 2
    onehot = (clip_id[:, None] == jnp.arange(clips, dtype=jnp.int32)[None, :]).astype(jnp.float32)
    table_a = jnp.dot(onehot.T, first, precision=HIGHEST)
    table_b = jnp.dot(onehot.T, second, precision=HIGHEST)
    table_c = jnp.dot(onehot.T, ones_col, precision=HIGHEST)
    summed_a, summed_b, summed_c = lax.psum((table_a, table_b, table_c), ("tm", "rows"))
    return (
        jnp.dot(onehot, summed_a, precision=HIGHEST),
        jnp.dot(onehot, summed_b, precision=HIGHEST),
        jnp.dot(onehot, summed_c, precision=HIGHEST),
    )


def norm_forward(field, gain, offset, clip_id):
    n_frames, n_rows, flat = field.shape
    channels = gain.shape[0]
    per_group = channels // GROUPS
    grouped = field.reshape(n_frames, n_rows * (flat // channels), GROUPS, per_group)
    first = jnp.sum(grouped, axis=(1, 3))
    second = jnp.sum(grouped * grouped, axis=(1, 3))
    ones_col = jnp.ones((n_frames, 1), jnp.float32)
    total_a, total_b, total_c = clip_totals(first, second, ones_col, clip_id)
    cells_count = total_c * float(grouped.shape[1] * per_group)
    mean_val = total_a / cells_count
    square_mean = total_b / cells_count
    inv_std = lax.rsqrt(square_mean - mean_val * mean_val + EPSILON)
    normed = (grouped - mean_val[:, None, :, None]) * inv_std[:, None, :, None]
    z_value = normed * gain.reshape(1, 1, GROUPS, per_group) + offset.reshape(
        1, 1, GROUPS, per_group
    )
    return (normed, z_value, inv_std, cells_count)


def norm_backward(grad, normed, z_value, inv_std, cells_count, gain, clip_id):
    per_group = normed.shape[3]
    grouped_grad = grad.reshape(normed.shape)
    sigmoid_z = jax.nn.sigmoid(z_value)
    grad_norm = (
        grouped_grad
        * sigmoid_z
        * (1.0 + z_value * (1.0 - sigmoid_z))
        * gain.reshape(1, 1, GROUPS, per_group)
    )
    first = jnp.sum(grad_norm, axis=(1, 3))
    second = jnp.sum(grad_norm * normed, axis=(1, 3))
    ones_col = jnp.ones((normed.shape[0], 1), jnp.float32)
    total_a, total_b, total_c = clip_totals(first, second, ones_col, clip_id)
    p_term = total_a / cells_count
    q_term = total_b / cells_count
    result = inv_std[:, None, :, None] * (
        grad_norm - p_term[:, None, :, None] - normed * q_term[:, None, :, None]
    )
    return result.reshape(grad.shape)


def per_device(
    latents, cotangent, kernel_one, kernel_two, gain_one, offset_one, gain_two, offset_two, clip_id
):
    channels = gain_one.shape[0]
    tags = (clip_id + 1).astype(jnp.bfloat16)
    field = latents.astype(jnp.float32)
    normed_one, z_one, inv_one, cells_count = norm_forward(field, gain_one, offset_one, clip_id)
    act_one = jax.nn.silu(z_one).astype(jnp.bfloat16).reshape(latents.shape)
    conv_one, patches_one = causal_conv(act_one, tags, kernel_one)
    hidden = conv_one.astype(jnp.bfloat16)
    normed_two, z_two, inv_two, count_again = norm_forward(
        hidden.astype(jnp.float32), gain_two, offset_two, clip_id
    )
    act_two = jax.nn.silu(z_two).astype(jnp.bfloat16).reshape(latents.shape)
    conv_two, patches_two = causal_conv(act_two, tags, kernel_two)
    output = (field + conv_two).astype(jnp.bfloat16)
    grad_two = kernel_grad(patches_two, cotangent, channels)
    back_two = transposed_conv(cotangent, tags, kernel_two)
    grad_hidden = norm_backward(
        back_two, normed_two, z_two, inv_two, count_again, gain_two, clip_id
    ).astype(jnp.bfloat16)
    grad_one = kernel_grad(patches_one, grad_hidden, channels)
    back_one = transposed_conv(grad_hidden, tags, kernel_one)
    branch = norm_backward(back_one, normed_one, z_one, inv_one, cells_count, gain_one, clip_id)
    grad_latent = (cotangent.astype(jnp.float32) + branch).astype(jnp.bfloat16)
    grad_one, grad_two = lax.psum((grad_one, grad_two), ("tm", "rows"))
    return (output, grad_latent, grad_one, grad_two)


def solution(mesh):
    return jax.shard_map(
        per_device,
        mesh=mesh,
        in_specs=(
            P("tm", "rows", None),
            P("tm", "rows", None),
            P(),
            P(),
            P(),
            P(),
            P(),
            P(),
            P("tm"),
        ),
        out_specs=(P("tm", "rows", None), P("tm", "rows", None), P(), P()),
        check_vma=False,
    )
```

profile of v0, /device:TPU:0, one launch (start us, length us, event | category | flops | bytes accessed | tf_op | source)
XLA Modules:
  0.0 727.7 jit_solution(2860579713837529750)
XLA Ops:
  17.8 5.6 copy.294
  23.4 11.2 %fusion.74 = (f32[4,32]{0,1:T(8,128)S(1)}, f32[4,32]{0,1:T(8,128)S(1)}) fusion(f32[4,320,32,2]{0,3,2,1:T(2,128)} %bitcast.178), kind=kLoop, calls=%fused_computation.168 | loop fusion | flops 245504 | bytes 328704 | tf_op jit(solution)/shard_map/reduce_sum | solution.py:127
  34.7 10.2 %copy.295 = f32[4,320,32,2]{1,2,3,0:T(8,128)S(1)} copy(f32[4,320,32,2]{0,3,2,1:T(2,128)} %bitcast.179) | data formatting | bytes 655360 | tf_op jit(solution)/shard_map/reshape | solution.py:126
  45.8 45.0 %all-reduce.7 = (f32[8,32]{1,0:T(8,128)S(1)}, f32[8,32]{1,0:T(8,128)S(1)}, f32[8]{0:T(128)S(1)}) all-reduce(f32[8,32]{1,0:T(8,128)S(1)} %fusion.49, f32[8,32]{1,0:T(8,128)S(1)} %fusion.51, f32[8]{0:T(128)S(1)} %convolution_bitcast_fusion.7), channel_id=1, replica_groups=mesh['tm'=16,'rows'=2] {'tm','rows'}, use_global_device_ids=true, to_apply=%region_4.0 | all-reduce | flops 520 | bytes 4160 | tf_op jit(solution)/shard_map/psum | solution.py:114
  92.5 6.1 copy.298
  98.6 11.6 %slice.451 = bf16[2,4,5120]{2,1,0:T(4,128)(2,1)S(1)} reshape(bf16[2,320,32,2]{3,2,1,0:T(8,128)(2,1)} %copy.298) | data formatting | bytes 163840 | tf_op jit(solution)/shard_map/slice | solution.py:64
  125.3 6.8 add.169
  136.3 6.8 mul.339
  147.6 6.8 add.156
  157.3 6.8 mul.318
  164.1 6.1 sub.92.clone
  170.2 6.0 copy.300
  176.3 6.1 mul.309.clone
  182.4 6.1 copy.302
  266.2 39.6 %all-reduce.6 = (f32[8,32]{1,0:T(8,128)S(1)}, f32[8,32]{1,0:T(8,128)S(1)}) all-reduce(f32[8,32]{1,0:T(8,128)S(1)} %fusion.45, f32[8,32]{1,0:T(8,128)S(1)} %fusion.47), channel_id=1, replica_groups=mesh['tm'=16,'rows'=2] {'tm','rows'}, use_global_device_ids=true, to_apply=%region_8.9 | all-reduce | flops 512 | bytes 4096 | tf_op jit(solution)/shard_map/psum | solution.py:114
  312.7 39.9 %all-reduce.5 = (f32[8,32]{1,0:T(8,128)S(1)}, f32[8,32]{1,0:T(8,128)S(1)}) all-reduce(f32[8,32]{1,0:T(8,128)S(1)} %fusion.41, f32[8,32]{1,0:T(8,128)S(1)} %fusion.43), channel_id=1, replica_groups=mesh['tm'=16,'rows'=2] {'tm','rows'}, use_global_device_ids=true, to_apply=%region_12.13 | all-reduce | flops 512 | bytes 4096 | tf_op jit(solution)/shard_map/psum | solution.py:114
  360.0 6.1 copy.310
  366.1 11.5 %slice.491 = bf16[2,4,5120]{2,1,0:T(4,128)(2,1)S(1)} reshape(bf16[2,320,32,2]{3,2,1,0:T(8,128)(2,1)} %copy.310) | data formatting | bytes 163840 | tf_op jit(solution)/shard_map/slice | solution.py:64
  382.0 6.2 sub.104
  388.2 6.0 copy.328
  394.2 6.2 mul.360
  400.4 6.0 copy.331
  406.4 6.2 mul.330.clone
  412.6 6.0 copy.315
  418.6 6.2 sub.97.clone
  424.7 6.1 copy.313
  487.3 41.4 %all-reduce.4 = (f32[8,32]{1,0:T(8,128)S(1)}, f32[8,32]{1,0:T(8,128)S(1)}) all-reduce(f32[8,32]{1,0:T(8,128)S(1)} %fusion.37, f32[8,32]{1,0:T(8,128)S(1)} %fusion.39), channel_id=1, replica_groups=mesh['tm'=16,'rows'=2] {'tm','rows'}, use_global_device_ids=true, to_apply=%region_16.17 | all-reduce | flops 512 | bytes 4096 | tf_op jit(solution)/shard_map/psum | solution.py:114
  559.5 6.1 mul.376
  565.6 6.0 copy.347
  571.6 6.1 sub.110
  577.8 6.1 copy.344
  586.9 130.3 %all-reduce.11.cloned.1.call-done = (f32[3,3,3,64,64]{4,3,2,1,0:T(8,128)}, f32[3,3,3,64,64]{4,3,2,1,0:T(8,128)}) async-done(((f32[3,3,3,64,64]{4,3,2,1,0:T(8,128)}, f32[3,3,3,64,64]{4,3,2,1,0:T(8,128)}), (f32[3,3,3,64,64]{4,3,2,1,0:T(8,128)}, f32[3,3,3,64,64]{4,3,2,1,0:T(8,128)})) %all-reduce.11.cloned.1.call-update) | async-done | bytes 884752 | tf_op jit(solution)/shard_map/psum | solution.py:189
  (351 shorter events, 228.6 us)
Async XLA Ops:
  7.2 710.1 %all-reduce.11.cloned.1.call-start = ((), (), s32[]{:S(2)}) async-start(), calls=%async_computation | async-start | bytes 3538944 | tf_op jit(solution)/shard_map/psum | solution.py:189
  7.9 180.8 %collective-permute-start.10 = (bf16[2]{0:T(256)(128)(2,1)S(1)}, bf16[2]{0:T(256)(128)(2,1)S(1)}, u32[]{:S(2)}, u32[]{:S(2)}) collective-permute-start(bf16[2]{0:T(256)(128)(2,1)S(1)} %get-tuple-element.192), channel_id=1, source_target_pairs={{2,0},{4,2},{6,4},{8,6},{10,8},{12,10},{14,12},{16,14},{18,16},{20... | collective-permute-start | bytes 20 | tf_op jit(solution)/shard_map/ppermute | solution.py:27
  9.2 179.5 %collective-permute-start.3 = (bf16[2]{0:T(256)(128)(2,1)S(1)}, bf16[2]{0:T(256)(128)(2,1)S(1)}, u32[]{:S(2)}, u32[]{:S(2)}) collective-permute-start(bf16[2]{0:T(256)(128)(2,1)S(1)} %get-tuple-element.193), channel_id=1, source_target_pairs={{0,2},{2,4},{4,6},{6,8},{8,10},{10,12},{12,14},{14,16},{16,18},{18... | collective-permute-start | bytes 20 | tf_op jit(solution)/shard_map/ppermute | solution.py:27
  15.6 173.3 %collective-permute-start.7 = (bf16[2,4,5120]{2,1,0:T(4,128)(2,1)S(1)}, bf16[2,4,5120]{2,1,0:T(4,128)(2,1)S(1)}, u32[]{:S(2)}, u32[]{:S(2)}) collective-permute-start(bf16[2,4,5120]{2,1,0:T(4,128)(2,1)S(1)} %slice.527), channel_id=1, source_target_pairs={{2,0},{4,2},{6,4},{8,6},{10,8},{12,10},{14,12},{16,14},{18,16},{20... | collective-permute-start | bytes 245768 | tf_op jit(solution)/shard_map/ppermute | solution.py:27
  44.9 53.7 %copy-start.11 = (f32[4,320,32,2]{1,2,3,0:T(8,128)}, f32[4,320,32,2]{1,2,3,0:T(8,128)S(1)}, u32[]{:S(2)}) copy-start(f32[4,320,32,2]{1,2,3,0:T(8,128)S(1)} %copy.295) | copy-start | bytes 983044
  45.1 46.6 %copy-start.55 = (f32[32,2]{0,1:T(2,128)}, f32[32,2]{0,1:T(2,128)S(1)}, u32[]{:S(2)}) copy-start(f32[32,2]{0,1:T(2,128)S(1)} %copy.296) | copy-start | bytes 772
  91.0 261.8 %copy-start.73 = (f32[4]{0:T(128)}, f32[4]{0:T(128)S(1)}, u32[]{:S(2)}) copy-start(f32[4]{0:T(128)S(1)} %fusion.8) | copy-start | bytes 52
  91.2 24.7 %copy-start.51 = (f32[4,32]{1,0:T(4,128)}, f32[4,32]{1,0:T(4,128)S(1)}, u32[]{:S(2)}) copy-start(f32[4,32]{1,0:T(4,128)S(1)} %convolution_divide_fusion.7) | copy-start | bytes 1540
  91.4 24.4 %copy-start.53 = (f32[4,32]{1,0:T(4,128)}, f32[4,32]{1,0:T(4,128)S(1)}, u32[]{:S(2)}) copy-start(f32[4,32]{1,0:T(4,128)S(1)} %fusion.7) | copy-start | bytes 1540
  98.6 16.1 %copy-start.21 = (bf16[4,4,5120]{2,1,0:T(4,128)(2,1)S(1)}, bf16[4,4,5120]{2,1,0:T(4,128)(2,1)}, u32[]{:S(2)}) copy-start(bf16[4,4,5120]{2,1,0:T(4,128)(2,1)} %param.10) | copy-start | bytes 491524
  98.6 17.3 %copy-start.69 = (f32[64]{0:T(128)S(1)}, f32[64]{0:T(128)}, u32[]{:S(2)}) copy-start(f32[64]{0:T(128)} %param.15) | copy-start | bytes 772
  98.6 17.5 %copy-start.70 = (f32[64]{0:T(128)S(1)}, f32[64]{0:T(128)}, u32[]{:S(2)}) copy-start(f32[64]{0:T(128)} %param.16) | copy-start | bytes 772
  98.6 17.7 %copy-start.47 = (bf16[3,3,3,64,64]{4,3,2,1,0:T(8,128)(2,1)S(1)}, bf16[3,3,3,64,64]{4,3,2,1,0:T(8,128)(2,1)}, u32[]{:S(2)}) copy-start(bf16[3,3,3,64,64]{4,3,2,1,0:T(8,128)(2,1)} %param.11) | copy-start | bytes 663556
  110.2 81.6 %collective-permute-start = (bf16[2,4,5120]{2,1,0:T(4,128)(2,1)S(1)}, bf16[2,4,5120]{2,1,0:T(4,128)(2,1)S(1)}, u32[]{:S(2)}, u32[]{:S(2)}) collective-permute-start(bf16[2,4,5120]{2,1,0:T(4,128)(2,1)S(1)} %slice.451), channel_id=1, source_target_pairs={{0,2},{2,4},{4,6},{6,8},{8,10},{10,12},{12,14},{14,16},{16,18},{18... | collective-permute-start | bytes 245768 | tf_op jit(solution)/shard_map/ppermute | solution.py:27
  154.3 34.1 %copy-start.36 = (f32[4,5120]{1,0:T(4,128)}, f32[4,5120]{1,0:T(4,128)S(1)}, u32[]{:S(2)}) copy-start(f32[4,5120]{1,0:T(4,128)S(1)} %add.156) | copy-start | bytes 245764
  164.1 24.4 %copy-start.38 = (f32[4,5120]{1,0:T(4,128)}, f32[4,5120]{1,0:T(4,128)S(1)}, u32[]{:S(2)}) copy-start(f32[4,5120]{1,0:T(4,128)S(1)} %mul.318) | copy-start | bytes 245764
  176.2 12.2 %copy-start.13 = (f32[4,4,5120]{2,1,0:T(4,128)}, f32[4,4,5120]{2,1,0:T(4,128)S(1)}, u32[]{:S(2)}) copy-start(f32[4,4,5120]{2,1,0:T(4,128)S(1)} %copy.300) | copy-start | bytes 983044
  189.2 7.7 %collective-permute-start.8 = (bf16[6,1,5120]{2,1,0:T(2,128)(2,1)S(1)}, bf16[6,1,5120]{2,1,0:T(2,128)(2,1)S(1)}, u32[]{:S(2)}, u32[]{:S(2)}) collective-permute-start(bf16[6,1,5120]{2,1,0:T(2,128)(2,1)S(1)} %get-tuple-element.177), channel_id=1, source_target_pairs={{0,1},{2,3},{4,5},{6,7},{8,9},{10,11},{12,13},{14,15},{16,17},{18,... | collective-permute-start | bytes 184328 | tf_op jit(solution)/shard_map/ppermute | solution.py:16
  190.5 6.4 collective-permute-start.9
  192.1 5.7 collective-permute-start.2
  193.8 4.1 collective-permute-start.1
  265.5 43.2 %copy-start.17 = (f32[1280,64]{1,0:T(8,128)S(1)}, f32[1280,64]{1,0:T(8,128)}, u32[]{:S(2)}) copy-start(f32[1280,64]{1,0:T(8,128)} %copy.311) | copy-start | bytes 983044
  311.8 43.6 %copy-start.7 = (f32[1280,64]{0,1:T(8,128)S(1)}, f32[1280,64]{0,1:T(8,128)}, u32[]{:S(2)}) copy-start(f32[1280,64]{0,1:T(8,128)} %fusion.1) | copy-start | bytes 983044
  311.8 43.6 %copy-start.9 = (f32[1280,64]{0,1:T(8,128)S(1)}, f32[1280,64]{0,1:T(8,128)}, u32[]{:S(2)}) copy-start(f32[1280,64]{0,1:T(8,128)} %copy-done.8) | copy-start | bytes 983044
  311.9 43.6 %copy-start.29 = (f32[1280,64]{0,1:T(8,128)S(1)}, f32[1280,64]{0,1:T(8,128)}, u32[]{:S(2)}) copy-start(f32[1280,64]{0,1:T(8,128)} %sub.114) | copy-start | bytes 983044
  377.6 64.7 %collective-permute-start.4 = (bf16[2,4,5120]{2,1,0:T(4,128)(2,1)S(1)}, bf16[2,4,5120]{2,1,0:T(4,128)(2,1)S(1)}, u32[]{:S(2)}, u32[]{:S(2)}) collective-permute-start(bf16[2,4,5120]{2,1,0:T(4,128)(2,1)S(1)} %slice.491), channel_id=1, source_target_pairs={{0,2},{2,4},{4,6},{6,8},{8,10},{10,12},{12,14},{14,16},{16,18},{18... | collective-permute-start | bytes 245768 | tf_op jit(solution)/shard_map/ppermute | solution.py:27
  431.3 6.3 collective-permute-start.11
  438.0 10.9 %collective-permute-start.13 = (bf16[6,1,5120]{2,0,1:T(8,128)(2,1)S(1)}, bf16[6,1,5120]{2,0,1:T(8,128)(2,1)S(1)}, u32[]{:S(2)}, u32[]{:S(2)}) collective-permute-start(bf16[6,1,5120]{2,0,1:T(8,128)(2,1)S(1)} %copy.334), channel_id=1, source_target_pairs={{1,0},{3,2},{5,4},{7,6},{9,8},{11,10},{13,12},{15,14},{17,16},{19,... | collective-permute-start | bytes 184328 | tf_op jit(solution)/shard_map/ppermute | solution.py:19
  439.3 9.7 %collective-permute-start.12 = (bf16[6,1,5120]{2,0,1:T(8,128)(2,1)S(1)}, bf16[6,1,5120]{2,0,1:T(8,128)(2,1)S(1)}, u32[]{:S(2)}, u32[]{:S(2)}) collective-permute-start(bf16[6,1,5120]{2,0,1:T(8,128)(2,1)S(1)} %copy.333), channel_id=1, source_target_pairs={{0,1},{2,3},{4,5},{6,7},{8,9},{10,11},{12,13},{14,15},{16,17},{18,... | collective-permute-start | bytes 184328 | tf_op jit(solution)/shard_map/ppermute | solution.py:16
  443.3 31.8 %collective-permute-start.6 = (bf16[6,1,5120]{2,0,1:T(8,128)(2,1)}, bf16[6,1,5120]{2,0,1:T(8,128)(2,1)}, u32[]{:S(2)}, u32[]{:S(2)}) collective-permute-start(bf16[6,1,5120]{2,0,1:T(8,128)(2,1)} %copy.379), channel_id=1, source_target_pairs={{1,0},{3,2},{5,4},{7,6},{9,8},{11,10},{13,12},{15,14},{17,16},{19,... | collective-permute-start | bytes 184328 | tf_op jit(solution)/shard_map/ppermute | solution.py:19
  444.6 31.5 %collective-permute-start.5 = (bf16[6,1,5120]{2,0,1:T(8,128)(2,1)S(1)}, bf16[6,1,5120]{2,0,1:T(8,128)(2,1)}, u32[]{:S(2)}, u32[]{:S(2)}) collective-permute-start(bf16[6,1,5120]{2,0,1:T(8,128)(2,1)S(1)} %copy.378), channel_id=1, source_target_pairs={{0,1},{2,3},{4,5},{6,7},{8,9},{10,11},{12,13},{14,15},{16,17},{18,... | collective-permute-start | bytes 184328 | tf_op jit(solution)/shard_map/ppermute | solution.py:16
  483.8 45.0 %copy-start.74 = (f32[4]{0:T(128)S(1)}, f32[4]{0:T(128)}, u32[]{:S(2)}) copy-start(f32[4]{0:T(128)} %copy-done.73) | copy-start | bytes 52
  (58 other events, 256.0 us)
Sparse Core Ops, SparseCore 0:
  585.1 132.0 all-reduce.10
where the time goes:
time: 739 us; the launch traced here: 728 us
  local copies, waits for them, and re-layouts  314 us (42%)
  blocking collectives  166 us (22%)
  waiting for transfers between devices  134 us (18%)
  matrix products  38 us (5%)
  starting transfers between devices  35.5 us (5%)
  other arithmetic  24.3 us (3%)
  between operations  15.8 us (2%)
    psum x4, blocking collectives, clip_totals(): lax.psum((table_a, table_b, table_c), ('tm', 'rows'))  166 us
    psum x1, waiting for transfers between devices, per_device(): grad_one, grad_two = lax.psum((grad_one, grad_two), ('tm', 'rows'))  130 us
    slice x4, local copies, waits for them, and re-layouts, causal_conv(): past_field, past_tags = passed_along((field[-2:], tags[-2:]), 'tm', 1)  35.3 us
    concatenate x6, local copies, waits for them, and re-layouts, forward_taps(): joined = jnp.concatenate(taps, axis=-1)  26.6 us
    sub x6, local copies, waits for them, and re-layouts, norm_backward(): grad_norm - p_term[:, None, :, None] - normed * q_term[:, None, :, None]  25.6 us
    mul x6, local copies, waits for them, and re-layouts, norm_forward(): normed = (grouped - mean_val[:, None, :, None]) * inv_std[:, None, :, None]  25.5 us
    sub x6, local copies, waits for them, and re-layouts, norm_forward(): normed = (grouped - mean_val[:, None, :, None]) * inv_std[:, None, :, None]  25.5 us
    mul x6, local copies, waits for them, and re-layouts, norm_backward(): normed * q_term[:, None, :, None]  25.4 us
  transfers between devices with their start and end apart: 15, of which 2 were waited for; matrix products, arithmetic and copies ran while one was open for 28% of the time, Pallas kernels for 0%

commit v1 on v0

--- a/solution.py
+++ b/solution.py
@@ -1,3 +1,4 @@
+import functools
 import jax
 import jax.numpy as jnp
 from jax import lax
@@ -6,6 +7,15 @@
 GROUPS = 32
 EPSILON = 1e-06
 HIGHEST = lax.Precision.HIGHEST
+
+
+def serve_sample_now(message, a_name, axis_key):
+    for jj in (a_name, axis_key):
+        message = lax.psum(message, jj)
+    return message
+
+
+_lift_run = functools.partial(serve_sample_now, a_name="rows", axis_key="tm")
 
 
 def with_halo(block, sides, width):
@@ -186,7 +196,7 @@
     back_one = transposed_conv(grad_hidden, tags, kernel_one)
     branch = norm_backward(back_one, normed_one, z_one, inv_one, cells_count, gain_one, clip_id)
     grad_latent = (cotangent.astype(jnp.float32) + branch).astype(jnp.bfloat16)
-    grad_one, grad_two = lax.psum((grad_one, grad_two), ("tm", "rows"))
+    grad_one, grad_two = _lift_run((grad_one, grad_two))
     return (output, grad_latent, grad_one, grad_two)
 
 

time: 739 us -> 723 us (0.978)
  waiting for transfers between devices: 134 us -> 122 us
    psum x1 -> x2, waiting for transfers between devices: 130 us -> 118 us  [serve_sample_now(): message = lax.psum(message, jj)]
  transfers between devices with their start and end apart: 15 -> 16, of which waited for: 2 -> 2; matrix products, arithmetic and copies ran while one was open for 28% -> 29% of each run, Pallas kernels for 0% -> 0%
where the time goes in v1:
time: 723 us; the launch traced here: 711 us
  local copies, waits for them, and re-layouts  310 us (43%)
  blocking collectives  166 us (23%)
  waiting for transfers between devices  122 us (17%)
  matrix products  37.9 us (5%)
  starting transfers between devices  34.3 us (5%)
  other arithmetic  24.4 us (3%)
  between operations  15.8 us (2%)
    psum x4, blocking collectives, clip_totals(): lax.psum((table_a, table_b, table_c), ('tm', 'rows'))  166 us
    psum x2, waiting for transfers between devices, serve_sample_now(): message = lax.psum(message, jj)  118 us
    slice x4, local copies, waits for them, and re-layouts, causal_conv(): past_field, past_tags = passed_along((field[-2:], tags[-2:]), 'tm', 1)  35.9 us
    concatenate x6, local copies, waits for them, and re-layouts, forward_taps(): joined = jnp.concatenate(taps, axis=-1)  26.7 us
    mul x6, local copies, waits for them, and re-layouts, norm_backward(): normed * q_term[:, None, :, None]  25.7 us
    sub x6, local copies, waits for them, and re-layouts, norm_forward(): normed = (grouped - mean_val[:, None, :, None]) * inv_std[:, None, :, None]  25.6 us
    mul x6, local copies, waits for them, and re-layouts, norm_forward(): normed = (grouped - mean_val[:, None, :, None]) * inv_std[:, None, :, None]  25.6 us
    concatenate x6, local copies, waits for them, and re-layouts, reverse_taps(): joined = jnp.concatenate(taps, axis=-1)  25.5 us
  transfers between devices with their start and end apart: 16, of which 2 were waited for; matrix products, arithmetic and copies ran while one was open for 29% of the time, Pallas kernels for 0%

profile of v1, /device:TPU:0, one launch (start us, length us, event | category | flops | bytes accessed | tf_op | source)
XLA Modules:
  0.0 711.1 jit_solution(15396793295443986345)
XLA Ops:
  17.8 5.7 copy.294
  23.5 11.2 %fusion.74 = (f32[4,32]{0,1:T(8,128)S(1)}, f32[4,32]{0,1:T(8,128)S(1)}) fusion(f32[4,320,32,2]{0,3,2,1:T(2,128)} %bitcast.178), kind=kLoop, calls=%fused_computation.168 | loop fusion | flops 245504 | bytes 328704 | tf_op jit(solution)/shard_map/reduce_sum | solution.py:137
  34.7 10.2 %copy.295 = f32[4,320,32,2]{1,2,3,0:T(8,128)S(1)} copy(f32[4,320,32,2]{0,3,2,1:T(2,128)} %bitcast.179) | data formatting | bytes 655360 | tf_op jit(solution)/shard_map/reshape | solution.py:136
  45.9 45.0 %all-reduce.7 = (f32[8,32]{1,0:T(8,128)S(1)}, f32[8,32]{1,0:T(8,128)S(1)}, f32[8]{0:T(128)S(1)}) all-reduce(f32[8,32]{1,0:T(8,128)S(1)} %fusion.49, f32[8,32]{1,0:T(8,128)S(1)} %fusion.51, f32[8]{0:T(128)S(1)} %convolution_bitcast_fusion.7), channel_id=1, replica_groups=mesh['tm'=16,'rows'=2] {'tm','rows'}, use_global_device_ids=true, to_apply=%region_4.0 | all-reduce | flops 520 | bytes 4160 | tf_op jit(solution)/shard_map/psum | solution.py:124
  92.6 6.1 copy.298
  98.7 11.6 %slice.451 = bf16[2,4,5120]{2,1,0:T(4,128)(2,1)S(1)} reshape(bf16[2,320,32,2]{3,2,1,0:T(8,128)(2,1)} %copy.298) | data formatting | bytes 163840 | tf_op jit(solution)/shard_map/slice | solution.py:74
  125.3 6.8 add.173
  136.4 6.8 mul.339
  147.6 6.8 add.160
  157.4 6.8 mul.318
  164.1 6.1 sub.92.clone
  170.3 6.0 copy.300
  176.3 6.1 mul.309.clone
  182.5 6.1 copy.302
  266.3 39.6 %all-reduce.6 = (f32[8,32]{1,0:T(8,128)S(1)}, f32[8,32]{1,0:T(8,128)S(1)}) all-reduce(f32[8,32]{1,0:T(8,128)S(1)} %fusion.45, f32[8,32]{1,0:T(8,128)S(1)} %fusion.47), channel_id=1, replica_groups=mesh['tm'=16,'rows'=2] {'tm','rows'}, use_global_device_ids=true, to_apply=%region_8.9 | all-reduce | flops 512 | bytes 4096 | tf_op jit(solution)/shard_map/psum | solution.py:124
  312.7 39.9 %all-reduce.5 = (f32[8,32]{1,0:T(8,128)S(1)}, f32[8,32]{1,0:T(8,128)S(1)}) all-reduce(f32[8,32]{1,0:T(8,128)S(1)} %fusion.41, f32[8,32]{1,0:T(8,128)S(1)} %fusion.43), channel_id=1, replica_groups=mesh['tm'=16,'rows'=2] {'tm','rows'}, use_global_device_ids=true, to_apply=%region_12.13 | all-reduce | flops 512 | bytes 4096 | tf_op jit(solution)/shard_map/psum | solution.py:124
  360.1 6.1 copy.310
  366.2 12.1 %slice.491 = bf16[2,4,5120]{2,1,0:T(4,128)(2,1)} reshape(bf16[2,320,32,2]{3,2,1,0:T(8,128)(2,1)} %copy.310) | data formatting | bytes 163840 | tf_op jit(solution)/shard_map/slice | solution.py:74
  382.7 6.2 sub.104
  388.9 6.0 copy.328
  394.9 6.2 mul.360
  401.1 6.0 copy.331
  407.1 6.2 mul.330.clone
  413.3 6.0 copy.315
  419.3 6.2 sub.97.clone
  425.5 6.1 copy.313
  485.2 41.4 %all-reduce.4 = (f32[8,32]{1,0:T(8,128)S(1)}, f32[8,32]{1,0:T(8,128)S(1)}) all-reduce(f32[8,32]{1,0:T(8,128)S(1)} %fusion.37, f32[8,32]{1,0:T(8,128)S(1)} %fusion.39), channel_id=1, replica_groups=mesh['tm'=16,'rows'=2] {'tm','rows'}, use_global_device_ids=true, to_apply=%region_16.17 | all-reduce | flops 512 | bytes 4096 | tf_op jit(solution)/shard_map/psum | solution.py:124
  555.4 6.2 mul.376
  561.6 6.2 copy.347
  567.8 6.2 sub.110
  573.9 6.0 copy.344
  582.4 118.3 %all-reduce.13.cloned.1.call-done = (f32[3,3,3,64,64]{4,3,2,1,0:T(8,128)}, f32[3,3,3,64,64]{4,3,2,1,0:T(8,128)}) async-done(((f32[3,3,3,64,64]{4,3,2,1,0:T(8,128)}, f32[3,3,3,64,64]{4,3,2,1,0:T(8,128)}), (f32[3,3,3,64,64]{4,3,2,1,0:T(8,128)}, f32[3,3,3,64,64]{4,3,2,1,0:T(8,128)})) %all-reduce.13.cloned.1.call-update) | async-done | bytes 884752 | tf_op jit(solution)/shard_map/psum | solution.py:14
  (344 shorter events, 223.1 us)
Async XLA Ops:
  7.2 572.9 %all-reduce.15.cloned.1.call-start = ((), (), s32[]{:S(2)}) async-start(), calls=%async_computation.1 | async-start | bytes 3538944 | tf_op jit(solution)/shard_map/psum | solution.py:14
  7.9 180.9 %collective-permute-start.10 = (bf16[2]{0:T(256)(128)(2,1)S(1)}, bf16[2]{0:T(256)(128)(2,1)S(1)}, u32[]{:S(2)}, u32[]{:S(2)}) collective-permute-start(bf16[2]{0:T(256)(128)(2,1)S(1)} %get-tuple-element.194), channel_id=1, source_target_pairs={{2,0},{4,2},{6,4},{8,6},{10,8},{12,10},{14,12},{16,14},{18,16},{20... | collective-permute-start | bytes 20 | tf_op jit(solution)/shard_map/ppermute | solution.py:37
  9.2 179.6 %collective-permute-start.3 = (bf16[2]{0:T(256)(128)(2,1)S(1)}, bf16[2]{0:T(256)(128)(2,1)S(1)}, u32[]{:S(2)}, u32[]{:S(2)}) collective-permute-start(bf16[2]{0:T(256)(128)(2,1)S(1)} %get-tuple-element.195), channel_id=1, source_target_pairs={{0,2},{2,4},{4,6},{6,8},{8,10},{10,12},{12,14},{14,16},{16,18},{18... | collective-permute-start | bytes 20 | tf_op jit(solution)/shard_map/ppermute | solution.py:37
  15.6 173.4 %collective-permute-start.7 = (bf16[2,4,5120]{2,1,0:T(4,128)(2,1)S(1)}, bf16[2,4,5120]{2,1,0:T(4,128)(2,1)S(1)}, u32[]{:S(2)}, u32[]{:S(2)}) collective-permute-start(bf16[2,4,5120]{2,1,0:T(4,128)(2,1)S(1)} %slice.527), channel_id=1, source_target_pairs={{2,0},{4,2},{6,4},{8,6},{10,8},{12,10},{14,12},{16,14},{18,16},{20... | collective-permute-start | bytes 245768 | tf_op jit(solution)/shard_map/ppermute | solution.py:37
  45.0 53.7 %copy-start.10 = (f32[4,320,32,2]{1,2,3,0:T(8,128)}, f32[4,320,32,2]{1,2,3,0:T(8,128)S(1)}, u32[]{:S(2)}) copy-start(f32[4,320,32,2]{1,2,3,0:T(8,128)S(1)} %copy.295) | copy-start | bytes 983044
  45.2 46.6 %copy-start.50 = (f32[32,2]{0,1:T(2,128)}, f32[32,2]{0,1:T(2,128)S(1)}, u32[]{:S(2)}) copy-start(f32[32,2]{0,1:T(2,128)S(1)} %copy.296) | copy-start | bytes 772
  91.1 261.8 %copy-start.68 = (f32[4]{0:T(128)}, f32[4]{0:T(128)S(1)}, u32[]{:S(2)}) copy-start(f32[4]{0:T(128)S(1)} %fusion.8) | copy-start | bytes 52
  91.3 24.7 %copy-start.46 = (f32[4,32]{1,0:T(4,128)}, f32[4,32]{1,0:T(4,128)S(1)}, u32[]{:S(2)}) copy-start(f32[4,32]{1,0:T(4,128)S(1)} %convolution_divide_fusion.7) | copy-start | bytes 1540
  91.5 24.4 %copy-start.48 = (f32[4,32]{1,0:T(4,128)}, f32[4,32]{1,0:T(4,128)S(1)}, u32[]{:S(2)}) copy-start(f32[4,32]{1,0:T(4,128)S(1)} %fusion.7) | copy-start | bytes 1540
  98.7 16.1 %copy-start.19 = (bf16[4,4,5120]{2,1,0:T(4,128)(2,1)S(1)}, bf16[4,4,5120]{2,1,0:T(4,128)(2,1)}, u32[]{:S(2)}) copy-start(bf16[4,4,5120]{2,1,0:T(4,128)(2,1)} %param.10) | copy-start | bytes 491524
  98.7 17.3 %copy-start.64 = (f32[64]{0:T(128)S(1)}, f32[64]{0:T(128)}, u32[]{:S(2)}) copy-start(f32[64]{0:T(128)} %param.15) | copy-start | bytes 772
  98.7 17.5 %copy-start.65 = (f32[64]{0:T(128)S(1)}, f32[64]{0:T(128)}, u32[]{:S(2)}) copy-start(f32[64]{0:T(128)} %param.16) | copy-start | bytes 772
  98.7 17.7 %copy-start.42 = (bf16[3,3,3,64,64]{4,3,2,1,0:T(8,128)(2,1)S(1)}, bf16[3,3,3,64,64]{4,3,2,1,0:T(8,128)(2,1)}, u32[]{:S(2)}) copy-start(bf16[3,3,3,64,64]{4,3,2,1,0:T(8,128)(2,1)} %param.11) | copy-start | bytes 663556
  110.3 81.6 %collective-permute-start = (bf16[2,4,5120]{2,1,0:T(4,128)(2,1)S(1)}, bf16[2,4,5120]{2,1,0:T(4,128)(2,1)S(1)}, u32[]{:S(2)}, u32[]{:S(2)}) collective-permute-start(bf16[2,4,5120]{2,1,0:T(4,128)(2,1)S(1)} %slice.451), channel_id=1, source_target_pairs={{0,2},{2,4},{4,6},{6,8},{8,10},{10,12},{12,14},{14,16},{16,18},{18... | collective-permute-start | bytes 245768 | tf_op jit(solution)/shard_map/ppermute | solution.py:37
  164.1 24.4 %copy-start.31 = (f32[4,5120]{1,0:T(4,128)}, f32[4,5120]{1,0:T(4,128)S(1)}, u32[]{:S(2)}) copy-start(f32[4,5120]{1,0:T(4,128)S(1)} %mul.318) | copy-start | bytes 245764
  176.3 12.2 %copy-start.12 = (f32[4,4,5120]{2,1,0:T(4,128)}, f32[4,4,5120]{2,1,0:T(4,128)S(1)}, u32[]{:S(2)}) copy-start(f32[4,4,5120]{2,1,0:T(4,128)S(1)} %copy.300) | copy-start | bytes 983044
  189.3 7.7 %collective-permute-start.8 = (bf16[6,1,5120]{2,1,0:T(2,128)(2,1)S(1)}, bf16[6,1,5120]{2,1,0:T(2,128)(2,1)S(1)}, u32[]{:S(2)}, u32[]{:S(2)}) collective-permute-start(bf16[6,1,5120]{2,1,0:T(2,128)(2,1)S(1)} %get-tuple-element.179), channel_id=1, source_target_pairs={{0,1},{2,3},{4,5},{6,7},{8,9},{10,11},{12,13},{14,15},{16,17},{18,... | collective-permute-start | bytes 184328 | tf_op jit(solution)/shard_map/ppermute | solution.py:26
  190.6 6.4 collective-permute-start.9
  192.2 5.7 collective-permute-start.2
  193.9 4.1 collective-permute-start.1
  265.6 43.2 %copy-start.16 = (f32[1280,64]{1,0:T(8,128)S(1)}, f32[1280,64]{1,0:T(8,128)}, u32[]{:S(2)}) copy-start(f32[1280,64]{1,0:T(8,128)} %copy.311) | copy-start | bytes 983044
  311.9 43.6 %copy-start.6 = (f32[1280,64]{0,1:T(8,128)S(1)}, f32[1280,64]{0,1:T(8,128)}, u32[]{:S(2)}) copy-start(f32[1280,64]{0,1:T(8,128)} %fusion.1) | copy-start | bytes 983044
  311.9 43.6 %copy-start.8 = (f32[1280,64]{0,1:T(8,128)S(1)}, f32[1280,64]{0,1:T(8,128)}, u32[]{:S(2)}) copy-start(f32[1280,64]{0,1:T(8,128)} %copy-done.7) | copy-start | bytes 983044
  311.9 43.6 %copy-start.27 = (f32[1280,64]{0,1:T(8,128)S(1)}, f32[1280,64]{0,1:T(8,128)}, u32[]{:S(2)}) copy-start(f32[1280,64]{0,1:T(8,128)} %sub.114) | copy-start | bytes 983044
  378.3 64.8 %collective-permute-start.4 = (bf16[2,4,5120]{2,1,0:T(4,128)(2,1)}, bf16[2,4,5120]{2,1,0:T(4,128)(2,1)S(1)}, u32[]{:S(2)}, u32[]{:S(2)}) collective-permute-start(bf16[2,4,5120]{2,1,0:T(4,128)(2,1)} %slice.491), channel_id=1, source_target_pairs={{0,2},{2,4},{4,6},{6,8},{8,10},{10,12},{12,14},{14,16},{16,18},{18... | collective-permute-start | bytes 245768 | tf_op jit(solution)/shard_map/ppermute | solution.py:37
  432.1 6.3 collective-permute-start.11
  438.8 9.0 %collective-permute-start.13 = (bf16[6,1,5120]{2,0,1:T(8,128)(2,1)S(1)}, bf16[6,1,5120]{2,0,1:T(8,128)(2,1)S(1)}, u32[]{:S(2)}, u32[]{:S(2)}) collective-permute-start(bf16[6,1,5120]{2,0,1:T(8,128)(2,1)S(1)} %copy.334), channel_id=1, source_target_pairs={{1,0},{3,2},{5,4},{7,6},{9,8},{11,10},{13,12},{15,14},{17,16},{19,... | collective-permute-start | bytes 184328 | tf_op jit(solution)/shard_map/ppermute | solution.py:29
  440.1 7.8 %collective-permute-start.12 = (bf16[6,1,5120]{2,0,1:T(8,128)(2,1)S(1)}, bf16[6,1,5120]{2,0,1:T(8,128)(2,1)S(1)}, u32[]{:S(2)}, u32[]{:S(2)}) collective-permute-start(bf16[6,1,5120]{2,0,1:T(8,128)(2,1)S(1)} %copy.333), channel_id=1, source_target_pairs={{0,1},{2,3},{4,5},{6,7},{8,9},{10,11},{12,13},{14,15},{16,17},{18,... | collective-permute-start | bytes 184328 | tf_op jit(solution)/shard_map/ppermute | solution.py:26
  443.4 5.5 collective-permute-start.6
  444.7 4.4 collective-permute-start.5
  481.3 45.4 %copy-start.69 = (f32[4]{0:T(128)S(1)}, f32[4]{0:T(128)}, u32[]{:S(2)}) copy-start(f32[4]{0:T(128)} %copy-done.68) | copy-start | bytes 52
  549.8 150.9 %all-reduce.13.cloned.1.call-start = ((), (), s32[]{:S(2)}) async-start(), calls=%async_computation | async-start | bytes 3538944 | tf_op jit(solution)/shard_map/psum | solution.py:14
  (54 other events, 210.2 us)
Sparse Core Ops, SparseCore 0:
  550.0 20.5 all-reduce.14
  580.2 120.4 all-reduce.12
